TPU v7x, 512 devices: a whole 4x8x8 slice. The times are simulated.
512 devices in a mesh: row: 16 (over z, core), col: 32 (over x, y).
Axes of the slice: x: 4, y: 8, z: 8, core: 2. Of those that a mesh axis runs over, the one named last changes fastest.
Arguments:
- tokens: bfloat16 [512, 8192], P('col', 'row'), may hold values from -24 to 24
- scales: float32 [8192], P('row'), may hold values from 0.25 to 4
- gate_weight: bfloat16 [8192, 16384], P('row', 'col'), may hold values from -0.0625 to 0.0625
- up_weight: bfloat16 [8192, 16384], P('row', 'col'), may hold values from -0.0625 to 0.0625
- down_weight: bfloat16 [16384, 8192], P('col', 'row'), may hold values from -0.046875 to 0.046875
- gate_mask: int32 [64, 128], P('row', 'col'), may hold values 0 or 1
- up_mask: int32 [64, 128], P('row', 'col'), may hold values 0 or 1
- down_mask: int32 [128, 64], P('col', 'row'), may hold values 0 or 1
- cotangent: bfloat16 [512, 8192], P('col', 'row'), may hold values from -4 to 4
Outputs:
- output: bfloat16 [512, 8192], P('col', 'row')
- input_grad: bfloat16 [512, 8192], P('col', 'row')
- gate_grad: bfloat16 [8192, 16384], P('row', 'col')
- up_grad: bfloat16 [8192, 16384], P('row', 'col')
- down_grad: bfloat16 [16384, 8192], P('col', 'row')
Inputs may be any that keep to these rules, and one draw needn't show every extreme that they name: gate_mask is 1 where a 128 x 128 tile of gate_weight is kept and 0 where it is pruned. up_mask is 1 where a tile of up_weight is kept and 0 where it is pruned. down_mask is 1 where a tile of down_weight is kept and 0 where it is pruned.
All inputs are finite; a program needn't handle non-finite values. No bound on the sum of `gate_mask` or of `up_mask` or of `down_mask` on one device may be relied on, other than what follows from the above.
Results may differ from a plain program's by a relative error of at most 0.039.
Values may be sent and summed in bfloat16 or wider, within the bound.
No kernel may reach another device: no remote copies, remote signals or barrier semaphores. Data moves between devices by JAX's collectives and lax.ppermute only.
A program may use at most 64 MiB of HBM per device.

v0:
```python
import jax
import jax.numpy as jnp
from jax import lax
from jax.sharding import PartitionSpec as P

D = 8192
TILE = 128
clip_ratio = 1.5


def expand(mask):
    return jnp.repeat(jnp.repeat(mask, TILE, axis=0), TILE, axis=1).astype(jnp.float32)


def contract_last(left, right):
    return lax.dot_general(
        left, right, (((1,), (1,)), ((), ())), preferred_element_type=jnp.float32
    )


def contract_first(left, right):
    return lax.dot_general(
        left, right, (((0,), (0,)), ((), ())), preferred_element_type=jnp.float32
    )


def clip_tokens(smoothed, squares):
    limits = clip_ratio * jnp.sqrt(squares / D + 1e-06)[:, None]
    squashed = jnp.tanh(smoothed / limits)
    return (squashed, (limits * squashed).astype(jnp.bfloat16))


def swiglu_parts(gate_pre):
    sigmoid_gate = jax.nn.sigmoid(gate_pre)
    silu_gate = gate_pre * sigmoid_gate
    return (sigmoid_gate, silu_gate)


def swiglu_grads(hidden_grad, gate_pre, up_pre):
    sigmoid_gate, silu_gate = swiglu_parts(gate_pre)
    gate_dir = (
        hidden_grad * up_pre * sigmoid_gate * (1.0 + gate_pre * (1.0 - sigmoid_gate))
    ).astype(jnp.bfloat16)
    up_dir = (hidden_grad * silu_gate).astype(jnp.bfloat16)
    return jnp.concatenate([gate_dir, up_dir], axis=1)


def per_device(
    tokens, scales, gate_weight, up_weight, down_weight, gate_mask, up_mask, down_mask, cotangent
):
    hidden_width = gate_weight.shape[1]
    gate_keep = expand(gate_mask)
    up_keep = expand(up_mask)
    down_keep = expand(down_mask)
    gate_kept = (scales[:, None] * gate_weight.astype(jnp.float32) * gate_keep).astype(jnp.bfloat16)
    up_kept = (scales[:, None] * up_weight.astype(jnp.float32) * up_keep).astype(jnp.bfloat16)
    down_kept = down_weight * down_keep.astype(jnp.bfloat16)
    both_kept = jnp.concatenate([gate_kept, up_kept], axis=1)
    smoothed = tokens.astype(jnp.float32) / scales
    squares = lax.psum(jnp.sum(smoothed * smoothed, axis=1), "row")
    squashed, quantized = clip_tokens(smoothed, squares)
    quantized_all = lax.all_gather(quantized, "col", axis=0, tiled=True)
    picked = quantized_all
    gate_up = lax.psum(
        jnp.dot(picked, both_kept, preferred_element_type=jnp.float32).astype(jnp.bfloat16), "row"
    ).astype(jnp.float32)
    gate_pre = gate_up[:, :hidden_width]
    up_pre = gate_up[:, hidden_width:]
    sigmoid_gate, silu_gate = swiglu_parts(gate_pre)
    hidden_all = (silu_gate * up_pre).astype(jnp.bfloat16)
    picked = hidden_all
    output = lax.psum_scatter(
        jnp.dot(picked, down_kept, preferred_element_type=jnp.float32).astype(jnp.bfloat16),
        "col",
        scatter_dimension=0,
        tiled=True,
    )
    cotangent_all = lax.all_gather(cotangent, "col", axis=0, tiled=True)
    down_grad = (contract_first(hidden_all, cotangent_all) * down_keep).astype(jnp.bfloat16)
    picked = cotangent_all
    hidden_grad = lax.psum(contract_last(picked, down_kept).astype(jnp.bfloat16), "row").astype(
        jnp.float32
    )
    both_dirs_all = swiglu_grads(hidden_grad, gate_pre, up_pre)
    picked = both_dirs_all
    quant_grad = lax.psum_scatter(
        contract_last(picked, both_kept).astype(jnp.bfloat16),
        "col",
        scatter_dimension=0,
        tiled=True,
    ).astype(jnp.float32)
    input_grad = (quant_grad * (1.0 - squashed * squashed) / scales).astype(jnp.bfloat16)
    weight_product = contract_first(quantized_all, both_dirs_all)
    gate_grad = (scales[:, None] * weight_product[:, :hidden_width] * gate_keep).astype(
        jnp.bfloat16
    )
    up_grad = (scales[:, None] * weight_product[:, hidden_width:] * up_keep).astype(jnp.bfloat16)
    return (output, input_grad, gate_grad, up_grad, down_grad)


def solution(mesh):
    placed = (
        P("col", "row"),
        P("row"),
        P("row", "col"),
        P("row", "col"),
        P("col", "row"),
        P("row", "col"),
        P("row", "col"),
        P("col", "row"),
        P("col", "row"),
    )
    return jax.shard_map(
        per_device,
        mesh=mesh,
        in_specs=placed,
        out_specs=(
            P("col", "row"),
            P("col", "row"),
            P("row", "col"),
            P("row", "col"),
            P("col", "row"),
        ),
        check_vma=False,
    )
```

profile of v0, /device:TPU:16, one launch (start us, length us, event | category | flops | bytes accessed | tf_op | source)
XLA Modules:
  0.0 713.3 jit_solution(10551113524191224439)
XLA Ops:
  7.2 0.0 copy-start.16
  7.2 0.0 all-reduce.3.cloned.1.call-start
  7.2 0.9 fusion.15
  8.1 32.0 %psum.21 = f32[16]{0:T(128)S(1)} all-reduce(f32[16]{0:T(128)S(1)} %fusion.15), channel_id=1, replica_groups=mesh['row'=16,'col'=32] {'row'}, use_global_device_ids=true, to_apply=%region_1.0 | all-reduce | flops 16 | bytes 128 | tf_op jit(solution)/shard_map/psum | solution.py:60
  40.1 0.7 convert_element_type.102
  40.8 0.7 convert_element_type.107
  41.5 0.7 convert_element_type.114
  42.2 0.8 multiply_convert_fusion.1
  43.0 50.1 %all_gather.6 = bf16[512,512]{1,0:T(8,128)(2,1)S(1)} all-gather(bf16[16,512]{1,0:T(8,128)(2,1)S(1)} %multiply_convert_fusion.1), channel_id=1, replica_groups=mesh['row'=16,'col'=32] {'col'}, dimensions={0}, use_global_device_ids=true | all-gather | bytes 540672 | tf_op jit(solution)/shard_map/all_gather | solution.py:62
  93.1 0.0 copy-start
  93.1 47.0 %all_gather.7 = bf16[512,512]{1,0:T(8,128)(2,1)S(1)} all-gather(bf16[16,512]{1,0:T(8,128)(2,1)} %param.17), channel_id=1, replica_groups=mesh['row'=16,'col'=32] {'col'}, dimensions={0}, use_global_device_ids=true | all-gather | bytes 540672 | tf_op jit(solution)/shard_map/all_gather | solution.py:78
  140.1 0.0 copy-start.2
  140.1 0.6 broadcast_in_dim.30
  140.7 0.0 copy-done.16
  140.7 1.3 fusion.1
  142.0 0.0 copy-start.7
  142.0 0.0 copy-start.8
  142.0 0.0 copy-start.15
  142.0 0.0 copy-done.2
  142.0 0.6 broadcast_in_dim.26
  142.7 0.6 broadcast_in_dim.28
  143.3 0.0 copy-done.7
  143.3 0.0 copy-done.8
  143.3 0.0 copy-done.15
  143.3 0.3 fusion.8
  143.6 0.0 copy-start.9
  143.6 0.0 copy-start.11
  143.6 0.0 copy-done
  143.7 0.8 copy-done.9
  144.4 0.2 copy-done.11
  144.6 1.7 convolution_convert_fusion
  146.3 0.0 all-reduce.3.cloned.1.call-update
  146.3 0.0 reduce-scatter.5.cloned.1.call-start
  146.4 114.4 %all-reduce.3.cloned.1.call-done = (bf16[512,1024]{1,0:T(8,128)(2,1)}, bf16[512,512]{1,0:T(8,128)(2,1)}) async-done(((bf16[512,1024]{1,0:T(8,128)(2,1)}, bf16[512,512]{1,0:T(8,128)(2,1)}), (bf16[512,1024]{1,0:T(8,128)(2,1)}, bf16[512,512]{1,0:T(8,128)(2,1)})) %all-reduce.3.cloned.1.call-update) | async-done | bytes 1572880 | tf_op jit(solution)/shard_map/psum | solution.py:64
  260.8 0.0 copy-start.13
  260.8 1.5 convert_element_type.112
  262.3 0.0 copy-done.13
  262.3 0.0 copy-start.10
  262.4 0.0 copy-start.12
  262.4 1.4 fusion.4
  263.8 0.0 copy-start.5
  263.8 0.8 copy-done.3
  264.6 0.2 copy-done.5
  264.8 0.0 copy-done.10
  264.8 0.0 copy-done.12
  264.8 1.6 convolution_convert_fusion.3
  266.4 0.0 reduce-scatter.5.cloned.1.call-update
  266.4 0.0 reduce-scatter.3.cloned.1.call-start
  266.4 2.5 convolution_convert_fusion.2
  268.9 0.0 reduce-scatter.3.cloned.1.call-update
  268.9 0.0 copy-start.1
  268.9 0.0 copy-start.4
  268.9 0.0 copy-start.6
  269.0 2.6 fusion
  271.5 0.0 copy-done.1
  271.5 0.0 copy-done.4
  271.5 0.0 copy-done.6
  271.5 0.7 fusion.11
  272.3 0.0 copy-start.14
  272.3 1.2 fusion.7
  273.5 210.9 %reduce-scatter.5.cloned.1.call-done = bf16[16,512]{1,0:T(8,128)(2,1)} async-done(((bf16[512,512]{1,0:T(8,128)(2,1)}), bf16[16,512]{1,0:T(8,128)(2,1)}) %reduce-scatter.5.cloned.1.call-update) | async-done | bytes 16400 | tf_op jit(solution)/shard_map/reduce_scatter | solution.py:86
  484.5 0.0 copy-done.14
  484.5 1.4 divide_convert_fusion
  485.9 220.9 %reduce-scatter.3.cloned.1.call-done = bf16[16,512]{1,0:T(8,128)(2,1)} async-done(((bf16[512,512]{1,0:T(8,128)(2,1)}), bf16[16,512]{1,0:T(8,128)(2,1)}) %reduce-scatter.3.cloned.1.call-update) | async-done | bytes 16400 | tf_op jit(solution)/shard_map/reduce_scatter | solution.py:72
  (5 shorter events, 0.1 us)
Async XLA Ops:
  7.2 133.6 %copy-start.16 = (bf16[512,512]{1,0:T(8,128)(2,1)S(1)}, bf16[512,512]{1,0:T(8,128)(2,1)}, u32[]{:S(2)}) copy-start(bf16[512,512]{1,0:T(8,128)(2,1)} %param.13) | copy-start | bytes 1572868
  7.2 253.6 %all-reduce.3.cloned.1.call-start = ((), (), s32[]{:S(2)}) async-start(), calls=%async_computation.4 | async-start | bytes 3145728 | tf_op jit(solution)/shard_map/psum | solution.py:64
  93.1 50.6 %copy-start = (bf16[512,512]{1,0:T(8,128)(2,1)}, bf16[512,512]{1,0:T(8,128)(2,1)S(1)}, u32[]{:S(2)}) copy-start(bf16[512,512]{1,0:T(8,128)(2,1)S(1)} %all_gather.6) | copy-start | bytes 1572868
  140.1 1.9 copy-start.2
  142.0 1.3 copy-start.7
  142.0 1.3 copy-start.8
  142.0 1.3 copy-start.15
  143.6 0.8 copy-start.9
  143.6 1.0 copy-start.11
  146.3 338.1 %reduce-scatter.5.cloned.1.call-start = ((), (), s32[]{:S(2)}) async-start(), calls=%async_computation.3 | async-start | bytes 540672 | tf_op jit(solution)/shard_map/reduce_scatter | solution.py:86
  260.8 1.5 copy-start.13
  262.3 2.4 copy-start.10
  262.4 2.4 copy-start.12
  263.8 0.8 copy-start.3
  263.8 1.0 copy-start.5
  266.4 440.4 %reduce-scatter.3.cloned.1.call-start = ((), (), s32[]{:S(2)}) async-start(), calls=%async_computation.2 | async-start | bytes 540672 | tf_op jit(solution)/shard_map/reduce_scatter | solution.py:72
  268.9 2.6 copy-start.1
  268.9 2.6 copy-start.4
  268.9 2.6 copy-start.6
  272.3 212.2 %copy-start.14 = (bf16[16,512]{1,0:T(8,128)(2,1)S(1)}, bf16[16,512]{1,0:T(8,128)(2,1)}, u32[]{:S(2)}) copy-start(bf16[16,512]{1,0:T(8,128)(2,1)} %param.9) | copy-start | bytes 49156
Sparse Core Ops, SparseCore 0:
  146.4 114.3 all-reduce.2
  266.5 217.9 reduce-scatter.4
  489.4 217.3 reduce-scatter.2
where the time goes:
time: 714 us; the launch traced here: 713 us
  waiting for transfers between devices  546 us (76%)
  blocking collectives  129 us (18%)
  between operations  13.9 us (2%)
  matrix products  10.3 us (1%)
  other arithmetic  9.67 us (1%)
    reduce_scatter x1, waiting for transfers between devices, per_device(): lax.psum_scatter(jnp.dot(picked, down_kept, preferred_element_type=jnp.fl...  221 us
    reduce_scatter x1, waiting for transfers between devices, per_device(): lax.psum_scatter(contract_last(picked, both_kept).astype(jnp.bfloat16), '...  211 us
    psum x1, waiting for transfers between devices, per_device(): lax.psum(jnp.dot(picked, both_kept, preferred_element_type=jnp.float32).a...  114 us
    all_gather x1, blocking collectives, per_device(): quantized_all = lax.all_gather(quantized, 'col', axis=0, tiled=True)  50.1 us
    all_gather x1, blocking collectives, per_device(): cotangent_all = lax.all_gather(cotangent, 'col', axis=0, tiled=True)  47 us
    psum x1, blocking collectives, per_device(): squares = lax.psum(jnp.sum(smoothed * smoothed, axis=1), 'row')  32 us
  transfers between devices with their start and end apart: 3, of which 3 were waited for; matrix products, arithmetic and copies ran while one was open for 1% of the time, Pallas kernels for 0%

commit v1 on v0

--- a/solution.py
+++ b/solution.py
@@ -59,7 +59,8 @@
     smoothed = tokens.astype(jnp.float32) / scales
     squares = lax.psum(jnp.sum(smoothed * smoothed, axis=1), "row")
     squashed, quantized = clip_tokens(smoothed, squares)
-    quantized_all = lax.all_gather(quantized, "col", axis=0, tiled=True)
+    stack = jnp.stack([quantized] * lax.axis_size("col"))
+    quantized_all = jnp.concatenate(lax.all_to_all(stack, "col", 0, 0), axis=0)
     picked = quantized_all
     gate_up = lax.psum(
         jnp.dot(picked, both_kept, preferred_element_type=jnp.float32).astype(jnp.bfloat16), "row"

time: 714 us -> 683 us (0.957)
  blocking collectives: 129 us -> 83.4 us
  starting transfers between devices: 0.12 us -> 10.2 us
    all_gather x1 -> x0, blocking collectives: 50.1 us -> none  [per_device(): quantized_all = lax.all_gather(quantized, 'col', axis=0, tiled=True)]
    all_to_all x0 -> x1, starting transfers between devices: none -> 10.1 us  [per_device(): quantized_all = jnp.concatenate(lax.all_to_all(stack, 'col', 0, 0), axis=0)]
  transfers between devices with their start and end apart: 3 -> 4, of which waited for: 3 -> 3; matrix products, arithmetic and copies ran while one was open for 1% -> 2% of each run, Pallas kernels for 0% -> 0%
where the time goes in v1:
time: 683 us; the launch traced here: 682 us
  waiting for transfers between devices  547 us (80%)
  blocking collectives  83.4 us (12%)
  between operations  13.9 us (2%)
  matrix products  12.6 us (2%)
  other arithmetic  10.7 us (2%)
  starting transfers between devices  10.2 us (1%)
    reduce_scatter x1, waiting for transfers between devices, per_device(): lax.psum_scatter(jnp.dot(picked, down_kept, preferred_element_type=jnp.fl...  221 us
    reduce_scatter x1, waiting for transfers between devices, per_device(): lax.psum_scatter(contract_last(picked, both_kept).astype(jnp.bfloat16), '...  210 us
    psum x1, waiting for transfers between devices, per_device(): lax.psum(jnp.dot(picked, both_kept, preferred_element_type=jnp.float32).a...  116 us
    all_gather x1, blocking collectives, per_device(): cotangent_all = lax.all_gather(cotangent, 'col', axis=0, tiled=True)  51.4 us
    psum x1, blocking collectives, per_device(): squares = lax.psum(jnp.sum(smoothed * smoothed, axis=1), 'row')  32 us
  transfers between devices with their start and end apart: 4, of which 3 were waited for; matrix products, arithmetic and copies ran while one was open for 2% of the time, Pallas kernels for 0%

profile of v1, /device:TPU:16, one launch (start us, length us, event | category | flops | bytes accessed | tf_op | source)
XLA Modules:
  0.0 682.1 jit_solution(1162408191164852506)
XLA Ops:
  7.2 0.0 copy-start.12
  7.2 0.9 fusion.15
  8.1 32.0 %psum.21 = f32[16]{0:T(128)S(1)} all-reduce(f32[16]{0:T(128)S(1)} %fusion.15), channel_id=1, replica_groups=mesh['row'=16,'col'=32] {'row'}, use_global_device_ids=true, to_apply=%region_1.0 | all-reduce | flops 16 | bytes 128 | tf_op jit(solution)/shard_map/psum | solution.py:60
  40.1 0.8 multiply_convert_fusion.1
  40.9 0.9 stack.2
  41.8 10.1 %all-to-all-start = ((bf16[32,16,512]{2,1,0:T(8,128)(2,1)}), bf16[32,16,512]{2,1,0:T(8,128)(2,1)}, u32[]{:S(2)}, u32[]{:S(2)}) async-start(bf16[32,16,512]{2,1,0:T(8,128)(2,1)} %stack.2), calls=%async_computation | async-start | bytes 1048576 | tf_op jit(solution)/shard_map/all_to_all | solution.py:63
  51.9 0.0 all-reduce.3.cloned.1.call-start
  51.9 0.7 convert_element_type.102
  52.6 0.7 convert_element_type.107
  53.3 0.7 convert_element_type.114
  54.0 51.4 %all_gather.3 = bf16[512,512]{1,0:T(8,128)(2,1)S(1)} all-gather(bf16[16,512]{1,0:T(8,128)(2,1)} %param.17), channel_id=1, replica_groups=mesh['row'=16,'col'=32] {'col'}, dimensions={0}, use_global_device_ids=true | all-gather | bytes 540672 | tf_op jit(solution)/shard_map/all_gather | solution.py:79
  105.4 0.0 copy-start
  105.4 0.6 broadcast_in_dim.30
  106.0 0.0 copy-done.12
  106.0 1.3 fusion.1
  107.3 0.0 copy-start.5
  107.3 0.0 copy-start.6
  107.3 0.0 copy-start.11
  107.3 0.0 copy-done
  107.3 0.6 broadcast_in_dim.26
  108.0 0.6 broadcast_in_dim.28
  108.6 0.0 copy-done.5
  108.6 0.0 copy-done.6
  108.6 0.0 copy-done.11
  108.6 1.3 fusion.8
  109.9 0.0 all-to-all-done
  109.9 3.1 convolution_convert_fusion
  112.9 0.0 all-reduce.3.cloned.1.call-update
  113.0 0.0 reduce-scatter.5.cloned.1.call-start
  113.0 116.4 %all-reduce.3.cloned.1.call-done = (bf16[512,1024]{1,0:T(8,128)(2,1)}, bf16[512,512]{1,0:T(8,128)(2,1)}) async-done(((bf16[512,1024]{1,0:T(8,128)(2,1)}, bf16[512,512]{1,0:T(8,128)(2,1)}), (bf16[512,1024]{1,0:T(8,128)(2,1)}, bf16[512,512]{1,0:T(8,128)(2,1)})) %all-reduce.3.cloned.1.call-update) | async-done | bytes 1572880 | tf_op jit(solution)/shard_map/psum | solution.py:65
  229.4 0.0 copy-start.9
  229.4 1.5 convert_element_type.112
  231.0 0.0 copy-done.9
  231.0 0.0 copy-start.7
  231.0 0.0 copy-start.8
  231.0 1.5 fusion.4
  232.5 0.0 copy-start.1
  232.5 0.0 copy-start.3
  232.5 0.8 copy-done.1
  233.3 0.1 copy-done.3
  233.5 0.0 copy-done.7
  233.5 0.0 copy-done.8
  233.5 1.5 convolution_convert_fusion.3
  235.0 0.0 reduce-scatter.5.cloned.1.call-update
  235.1 0.0 reduce-scatter.3.cloned.1.call-start
  235.1 2.4 convolution_convert_fusion.2
  237.6 0.0 reduce-scatter.3.cloned.1.call-update
  237.6 0.0 copy-start.2
  237.6 0.0 copy-start.4
  237.6 2.5 fusion
  240.1 0.0 copy-done.2
  240.1 0.0 copy-done.4
  240.1 1.8 fusion.11
  241.9 0.0 copy-start.10
  241.9 1.2 fusion.7
  243.2 210.0 %reduce-scatter.5.cloned.1.call-done = bf16[16,512]{1,0:T(8,128)(2,1)} async-done(((bf16[512,512]{1,0:T(8,128)(2,1)}), bf16[16,512]{1,0:T(8,128)(2,1)}) %reduce-scatter.5.cloned.1.call-update) | async-done | bytes 16400 | tf_op jit(solution)/shard_map/reduce_scatter | solution.py:87
  453.1 0.0 copy-done.10
  453.1 1.4 divide_convert_fusion
  454.6 221.0 %reduce-scatter.3.cloned.1.call-done = bf16[16,512]{1,0:T(8,128)(2,1)} async-done(((bf16[512,512]{1,0:T(8,128)(2,1)}), bf16[16,512]{1,0:T(8,128)(2,1)}) %reduce-scatter.3.cloned.1.call-update) | async-done | bytes 16400 | tf_op jit(solution)/shard_map/reduce_scatter | solution.py:73
  (4 shorter events, 0.1 us)
Async XLA Ops:
  7.2 98.8 %copy-start.12 = (bf16[512,512]{1,0:T(8,128)(2,1)S(1)}, bf16[512,512]{1,0:T(8,128)(2,1)}, u32[]{:S(2)}) copy-start(bf16[512,512]{1,0:T(8,128)(2,1)} %param.13) | copy-start | bytes 1572868
  41.8 68.1 %all-to-all-start = ((bf16[32,16,512]{2,1,0:T(8,128)(2,1)}), bf16[32,16,512]{2,1,0:T(8,128)(2,1)}, u32[]{:S(2)}, u32[]{:S(2)}) async-start(bf16[32,16,512]{2,1,0:T(8,128)(2,1)} %stack.2), calls=%async_computation | async-start | bytes 1048576 | tf_op jit(solution)/shard_map/all_to_all | solution.py:63
  51.9 177.6 %all-reduce.3.cloned.1.call-start = ((), (), s32[]{:S(2)}) async-start(), calls=%async_computation.5 | async-start | bytes 3145728 | tf_op jit(solution)/shard_map/psum | solution.py:65
  105.4 1.9 copy-start
  107.3 1.3 copy-start.5
  107.3 1.3 copy-start.6
  107.3 1.3 copy-start.11
  113.0 340.2 %reduce-scatter.5.cloned.1.call-start = ((), (), s32[]{:S(2)}) async-start(), calls=%async_computation.4 | async-start | bytes 540672 | tf_op jit(solution)/shard_map/reduce_scatter | solution.py:87
  229.4 1.5 copy-start.9
  231.0 2.5 copy-start.7
  231.0 2.5 copy-start.8
  232.5 0.8 copy-start.1
  232.5 1.0 copy-start.3
  235.1 440.5 %reduce-scatter.3.cloned.1.call-start = ((), (), s32[]{:S(2)}) async-start(), calls=%async_computation.3 | async-start | bytes 540672 | tf_op jit(solution)/shard_map/reduce_scatter | solution.py:73
  237.6 2.6 copy-start.2
  237.6 2.6 copy-start.4
  241.9 211.2 %copy-start.10 = (bf16[16,512]{1,0:T(8,128)(2,1)S(1)}, bf16[16,512]{1,0:T(8,128)(2,1)}, u32[]{:S(2)}) copy-start(bf16[16,512]{1,0:T(8,128)(2,1)} %param.9) | copy-start | bytes 49156
Sparse Core Ops, SparseCore 0:
  113.1 116.3 all-reduce.2
  235.2 217.9 reduce-scatter.4
  458.1 217.3 reduce-scatter.2
